TPU v7x, 256 devices: a whole 4x4x8 slice. The times are simulated.
256 devices in a mesh: layer: 2 (over z_lo), row: 8 (over y, core), col: 16 (over z_hi, x).
Axes of the slice: x: 4, y: 4, z: 8 (z_hi: 4, z_lo: 2; z = z_hi * 2 + z_lo), core: 2. Of those that a mesh axis runs over, the one named last changes fastest.
Arguments:
- matrix: float32 [16384, 16384], P('row', 'col'), may hold values from -1.5 to 1.5, as said below
Outputs:
- square_panel: float32 [16384, 512], P('row', 'layer')
- new_panel: float32 [16384, 512], P('row', 'layer')
Inputs may be any that keep to these rules, and one draw needn't show every extreme that they name: `matrix`: entries off the diagonal are of order 0.5 / sqrt(16384); the diagonal's magnitudes lie between 0.6 and 1 with either sign.
All inputs are finite; a program needn't handle non-finite values.
Results may differ from a plain program's by a relative error of at most 0.000076.
Values sent between devices are 32-bit elements; how exact they have to be, the bound alone decides.
A program may use at most 128 MiB of HBM per device.

v0:
```python
import jax
import jax.numpy as jnp
from jax import lax
from jax.sharding import PartitionSpec as P

PW = 512


def from_root(shard, axis, root):
    mine = lax.axis_index(axis) == root
    return lax.psum(jnp.where(mine, shard, jnp.zeros_like(shard)), axis)


def matmul_high(left_side, right_side):
    return jnp.dot(
        left_side, right_side, precision=lax.Precision.HIGHEST, preferred_element_type=jnp.float32
    )


def body(matrix):
    block_cols = matrix.shape[1]
    layers = lax.axis_size("layer")
    col_ratio = lax.axis_size("col") // lax.axis_size("row")
    col_index = lax.axis_index("col")
    layer_index = lax.axis_index("layer")
    half_width = PW // layers
    root_row = col_index // col_ratio
    offset = col_index % col_ratio * block_cols
    panel_full = from_root(matrix[:, :PW], "col", 0)
    own_cols = lax.dynamic_slice_in_dim(panel_full, layer_index * half_width, half_width, 1)
    depth_rows = block_cols // layers
    first_row = offset + layer_index * depth_rows
    panel_slab = from_root(
        lax.dynamic_slice_in_dim(panel_full, first_row, depth_rows, 0), "row", root_row
    )
    local_cols = lax.dynamic_slice_in_dim(matrix, layer_index * depth_rows, depth_rows, 1)
    square_full = lax.psum(matmul_high(local_cols, panel_slab), ("layer", "col"))
    square_slab = from_root(
        lax.dynamic_slice_in_dim(square_full, first_row, depth_rows, 0), "row", root_row
    )
    update = lax.psum_scatter(
        matmul_high(local_cols, square_slab), "layer", scatter_dimension=1, tiled=True
    )
    update = lax.psum(update, "col")
    square = lax.dynamic_slice_in_dim(square_full, layer_index * half_width, half_width, 1)
    new_panel = (3.0 * own_cols - update) * 0.5
    return (square, new_panel)


def solution(mesh):
    placed = (P("row", "col"),)
    return jax.shard_map(
        body,
        mesh=mesh,
        in_specs=placed,
        out_specs=(P("row", "layer"), P("row", "layer")),
        check_vma=False,
    )
```

profile of v0, /device:TPU:16, one launch (start us, length us, event | category | flops | bytes accessed | tf_op | source)
XLA Modules:
  0.0 809.4 jit_solution(460881230599396828)
XLA Ops:
  7.2 0.0 all-reduce.6.cloned.1.call-start
  7.2 4.6 slice_select_fusion
  11.9 0.0 all-reduce.6.cloned.1.call-update
  11.9 0.0 all-reduce.8.cloned.1.call-start
  12.0 224.7 %all-reduce.6.cloned.1.call-done = f32[2048,512]{1,0:T(8,128)} async-done(((f32[2048,512]{1,0:T(8,128)}), f32[2048,512]{1,0:T(8,128)}) %all-reduce.6.cloned.1.call-update) | async-done | bytes 4194320 | tf_op jit(solution)/shard_map/psum | solution.py:11
  236.6 2.3 dynamic-slice_select_fusion.1
  238.9 0.0 all-reduce.8.cloned.1.call-update
  239.0 0.0 all-reduce.10.cloned.1.call-start
  239.0 61.4 %all-reduce.8.cloned.1.call-done = f32[512,512]{1,0:T(8,128)} async-done(((f32[512,512]{1,0:T(8,128)}), f32[512,512]{1,0:T(8,128)}) %all-reduce.8.cloned.1.call-update) | async-done | bytes 1048592 | tf_op jit(solution)/shard_map/psum | solution.py:11
  300.4 10.1 %fusion.2 = f32[2048,512]{1,0:T(8,128)} fusion(f32[512,512]{1,0:T(8,128)} %all-reduce.8.cloned.1.call-done, f32[2048,1024]{1,0:T(8,128)} %param.1, s32[]{:T(128)S(6)} %select_n.42), kind=kOutput, calls=%fused_computation.3 | convolution fusion | flops 6442450944 | bytes 9437188 | tf_op jit(solution)/shard_map/dot_general | solution.py:15
  310.5 0.0 all-reduce.10.cloned.1.call-update
  310.5 0.0 all-reduce.12.cloned.1.call-start
  310.6 167.7 %all-reduce.10.cloned.1.call-done = f32[2048,512]{1,0:T(8,128)} async-done(((f32[2048,512]{1,0:T(8,128)}), f32[2048,512]{1,0:T(8,128)}) %all-reduce.10.cloned.1.call-update) | async-done | bytes 4194320 | tf_op jit(solution)/shard_map/psum | solution.py:37
  478.2 2.3 dynamic-slice_select_fusion
  480.5 0.0 all-reduce.12.cloned.1.call-update
  480.6 0.0 reduce-scatter.2.cloned.1.call-start
  480.6 61.5 %all-reduce.12.cloned.1.call-done = f32[512,512]{1,0:T(8,128)} async-done(((f32[512,512]{1,0:T(8,128)}), f32[512,512]{1,0:T(8,128)}) %all-reduce.12.cloned.1.call-update) | async-done | bytes 1048592 | tf_op jit(solution)/shard_map/psum | solution.py:11
  542.1 10.1 %fusion = f32[2048,512]{1,0:T(8,128)} fusion(f32[512,512]{1,0:T(8,128)} %all-reduce.12.cloned.1.call-done, f32[2048,1024]{1,0:T(8,128)} %param.1, s32[]{:T(128)S(6)} %select_n.42), kind=kOutput, calls=%fused_computation.1 | convolution fusion | flops 6442450944 | bytes 9437188 | tf_op jit(solution)/shard_map/dot_general | solution.py:15
  552.2 0.0 reduce-scatter.2.cloned.1.call-update
  552.2 0.0 all-reduce.14.cloned.1.call-start
  552.2 62.9 %reduce-scatter.2.cloned.1.call-done = f32[2048,256]{1,0:T(8,128)} async-done(((f32[2048,512]{1,0:T(8,128)}), f32[2048,256]{1,0:T(8,128)}) %reduce-scatter.2.cloned.1.call-update) | async-done | bytes 2097168 | tf_op jit(solution)/shard_map/reduce_scatter | solution.py:41
  615.2 3.0 constant_dynamic-slice_fusion
  618.3 180.5 %all-reduce.14.cloned.1.call-done = f32[2048,256]{1,0:T(8,128)} async-done(((f32[2048,256]{1,0:T(8,128)}), f32[2048,256]{1,0:T(8,128)}) %all-reduce.14.cloned.1.call-update) | async-done | bytes 2097168 | tf_op jit(solution)/shard_map/psum | solution.py:44
  798.7 3.8 subtract_multiply_fusion
  (1 shorter events, 0.0 us)
Async XLA Ops:
  7.2 229.5 %all-reduce.6.cloned.1.call-start = ((), (), s32[]{:S(2)}) async-start(), calls=%async_computation.1 | async-start | bytes 8388608 | tf_op jit(solution)/shard_map/psum | solution.py:11
  11.9 288.5 %all-reduce.8.cloned.1.call-start = ((), (), s32[]{:S(2)}) async-start(), calls=%async_computation.2 | async-start | bytes 2097152 | tf_op jit(solution)/shard_map/psum | solution.py:11
  239.0 239.3 %all-reduce.10.cloned.1.call-start = ((), (), s32[]{:S(2)}) async-start(), calls=%async_computation.3 | async-start | bytes 8388608 | tf_op jit(solution)/shard_map/psum | solution.py:37
  310.5 231.6 %all-reduce.12.cloned.1.call-start = ((), (), s32[]{:S(2)}) async-start(), calls=%async_computation.4 | async-start | bytes 2097152 | tf_op jit(solution)/shard_map/psum | solution.py:11
  480.6 134.6 %reduce-scatter.2.cloned.1.call-start = ((), (), s32[]{:S(2)}) async-start(), calls=%async_computation.5 | async-start | bytes 6291456 | tf_op jit(solution)/shard_map/reduce_scatter | solution.py:41
  552.2 246.5 %all-reduce.14.cloned.1.call-start = ((), (), s32[]{:S(2)}) async-start(), calls=%async_computation.6 | async-start | bytes 4194304 | tf_op jit(solution)/shard_map/psum | solution.py:44
Sparse Core Ops, SparseCore 0:
  12.0 224.5 all-reduce.5
  239.6 60.7 all-reduce.7
  310.6 167.5 all-reduce.9
  481.0 61.0 all-reduce.11
  552.3 62.8 reduce-scatter.1
  617.7 180.9 all-reduce.13
where the time goes:
time: 810 us; the launch traced here: 809 us
  waiting for transfers between devices  759 us (94%)
  matrix products  20.1 us (2%)
  between operations  14.2 us (2%)
  other arithmetic  13 us (2%)
    psum x3, waiting for transfers between devices, from_root(): return lax.psum(jnp.where(mine, shard, jnp.zeros_like(shard)), axis)  348 us
    psum x1, waiting for transfers between devices, body(): update = lax.psum(update, 'col')  180 us
    psum x1, waiting for transfers between devices, body(): lax.psum(matmul_high(local_cols, panel_slab), ('layer', 'col'))  168 us
    reduce_scatter x1, waiting for transfers between devices, body(): lax.psum_scatter(matmul_high(local_cols, square_slab), 'layer', scatter_d...  62.9 us
    dot_general x2, matrix products, matmul_high(): jnp.dot(left_side, right_side, precision=lax.Precision.HIGHEST, preferred...  20.1 us
  transfers between devices with their start and end apart: 6, of which 6 were waited for; matrix products, arithmetic and copies ran while one was open for 0% of the time, Pallas kernels for 0%

commit v1 on v0

--- a/solution.py
+++ b/solution.py
@@ -34,7 +34,7 @@
         lax.dynamic_slice_in_dim(panel_full, first_row, depth_rows, 0), "row", root_row
     )
     local_cols = lax.dynamic_slice_in_dim(matrix, layer_index * depth_rows, depth_rows, 1)
-    square_full = lax.psum(matmul_high(local_cols, panel_slab), ("layer", "col"))
+    square_full = lax.psum(lax.psum(matmul_high(local_cols, panel_slab), "col"), "layer")
     square_slab = from_root(
         lax.dynamic_slice_in_dim(square_full, first_row, depth_rows, 0), "row", root_row
     )

time: 810 us -> 988 us (1.22)
  waiting for transfers between devices: 759 us -> 937 us
    psum x1 -> x2, waiting for transfers between devices: 168 us -> 344 us  [the longest x1 225 us: body(): lax.psum(matmul_high(local_cols, panel_slab), 'col')]
  transfers between devices with their start and end apart: 6 -> 7, of which waited for: 6 -> 7; matrix products, arithmetic and copies ran while one was open for 0% -> 0% of each run, Pallas kernels for 0% -> 0%
where the time goes in v1:
time: 988 us
  waiting for transfers between devices  937 us (95%)
  matrix products  20.2 us (2%)
  between operations  14.2 us (1%)
  other arithmetic  13 us (1%)
    psum x3, waiting for transfers between devices, from_root(): return lax.psum(jnp.where(mine, shard, jnp.zeros_like(shard)), axis)  351 us
    psum x1, waiting for transfers between devices, body(): lax.psum(matmul_high(local_cols, panel_slab), 'col')  225 us
    psum x1, waiting for transfers between devices, body(): update = lax.psum(update, 'col')  179 us
    psum x1, waiting for transfers between devices, body(): lax.psum(lax.psum(matmul_high(local_cols, panel_slab), 'col'), 'layer')  119 us
    reduce_scatter x1, waiting for transfers between devices, body(): lax.psum_scatter(matmul_high(local_cols, square_slab), 'layer', scatter_d...  62.9 us
    dot_general x2, matrix products, matmul_high(): jnp.dot(left_side, right_side, precision=lax.Precision.HIGHEST, preferred...  20.2 us
  transfers between devices with their start and end apart: 7, of which 7 were waited for; matrix products, arithmetic and copies ran while one was open for 0% of the time, Pallas kernels for 0%

profile of v1, /device:TPU:16, one launch (start us, length us, event | category | flops | bytes accessed | tf_op | source)
XLA Modules:
  0.0 987.8 jit_solution(2636592461347693603)
XLA Ops:
  7.2 0.0 all-reduce.7.cloned.1.call-start
  7.2 4.6 slice_select_fusion
  11.9 0.0 all-reduce.7.cloned.1.call-update
  11.9 0.0 all-reduce.9.cloned.1.call-start
  12.0 224.7 %all-reduce.7.cloned.1.call-done = f32[2048,512]{1,0:T(8,128)} async-done(((f32[2048,512]{1,0:T(8,128)}), f32[2048,512]{1,0:T(8,128)}) %all-reduce.7.cloned.1.call-update) | async-done | bytes 4194320 | tf_op jit(solution)/shard_map/psum | solution.py:11
  236.6 2.3 dynamic-slice_select_fusion.1
  239.0 0.0 all-reduce.11.cloned.1.call-start
  239.0 61.4 %all-reduce.9.cloned.1.call-done = f32[512,512]{1,0:T(8,128)} async-done(((f32[512,512]{1,0:T(8,128)}), f32[512,512]{1,0:T(8,128)}) %all-reduce.9.cloned.1.call-update) | async-done | bytes 1048592 | tf_op jit(solution)/shard_map/psum | solution.py:11
  300.4 10.1 %fusion.2 = f32[2048,512]{1,0:T(8,128)} fusion(f32[512,512]{1,0:T(8,128)} %all-reduce.9.cloned.1.call-done, f32[2048,1024]{1,0:T(8,128)} %param.1, s32[]{:T(128)S(6)} %select_n.42), kind=kOutput, calls=%fused_computation.3 | convolution fusion | flops 6442450944 | bytes 9437188 | tf_op jit(solution)/shard_map/dot_general | solution.py:15
  310.5 0.0 all-reduce.11.cloned.1.call-update
  310.5 0.0 all-reduce.13.cloned.1.call-start
  310.6 225.2 %all-reduce.11.cloned.1.call-done = f32[2048,512]{1,0:T(8,128)} async-done(((f32[2048,512]{1,0:T(8,128)}), f32[2048,512]{1,0:T(8,128)}) %all-reduce.11.cloned.1.call-update) | async-done | bytes 4194320 | tf_op jit(solution)/shard_map/psum | solution.py:37
  535.8 0.0 all-reduce.13.cloned.1.call-update
  535.8 0.0 all-reduce.15.cloned.1.call-start
  535.9 118.7 %all-reduce.13.cloned.1.call-done = f32[2048,512]{1,0:T(8,128)} async-done(((f32[2048,512]{1,0:T(8,128)}), f32[2048,512]{1,0:T(8,128)}) %all-reduce.13.cloned.1.call-update) | async-done | bytes 4194320 | tf_op jit(solution)/shard_map/psum | solution.py:37
  654.5 2.3 dynamic-slice_select_fusion
  656.9 0.0 reduce-scatter.2.cloned.1.call-start
  656.9 64.7 %all-reduce.15.cloned.1.call-done = f32[512,512]{1,0:T(8,128)} async-done(((f32[512,512]{1,0:T(8,128)}), f32[512,512]{1,0:T(8,128)}) %all-reduce.15.cloned.1.call-update) | async-done | bytes 1048592 | tf_op jit(solution)/shard_map/psum | solution.py:11
  721.6 10.1 %fusion = f32[2048,512]{1,0:T(8,128)} fusion(f32[512,512]{1,0:T(8,128)} %all-reduce.15.cloned.1.call-done, f32[2048,1024]{1,0:T(8,128)} %param.1, s32[]{:T(128)S(6)} %select_n.42), kind=kOutput, calls=%fused_computation.1 | convolution fusion | flops 6442450944 | bytes 9437188 | tf_op jit(solution)/shard_map/dot_general | solution.py:15
  731.7 0.0 all-reduce.17.cloned.1.call-start
  731.7 62.9 %reduce-scatter.2.cloned.1.call-done = f32[2048,256]{1,0:T(8,128)} async-done(((f32[2048,512]{1,0:T(8,128)}), f32[2048,256]{1,0:T(8,128)}) %reduce-scatter.2.cloned.1.call-update) | async-done | bytes 2097168 | tf_op jit(solution)/shard_map/reduce_scatter | solution.py:41
  794.7 3.0 constant_dynamic-slice_fusion
  797.7 179.5 %all-reduce.17.cloned.1.call-done = f32[2048,256]{1,0:T(8,128)} async-done(((f32[2048,256]{1,0:T(8,128)}), f32[2048,256]{1,0:T(8,128)}) %all-reduce.17.cloned.1.call-update) | async-done | bytes 2097168 | tf_op jit(solution)/shard_map/psum | solution.py:44
  977.2 3.8 subtract_multiply_fusion
  (4 shorter events, 0.1 us)
Async XLA Ops:
  7.2 229.5 %all-reduce.7.cloned.1.call-start = ((), (), s32[]{:S(2)}) async-start(), calls=%async_computation.1 | async-start | bytes 8388608 | tf_op jit(solution)/shard_map/psum | solution.py:11
  11.9 288.5 %all-reduce.9.cloned.1.call-start = ((), (), s32[]{:S(2)}) async-start(), calls=%async_computation.2 | async-start | bytes 2097152 | tf_op jit(solution)/shard_map/psum | solution.py:11
  239.0 296.9 %all-reduce.11.cloned.1.call-start = ((), (), s32[]{:S(2)}) async-start(), calls=%async_computation.3 | async-start | bytes 8388608 | tf_op jit(solution)/shard_map/psum | solution.py:37
  310.5 344.0 %all-reduce.13.cloned.1.call-start = ((), (), s32[]{:S(2)}) async-start(), calls=%async_computation.4 | async-start | bytes 8388608 | tf_op jit(solution)/shard_map/psum | solution.py:37
  535.8 185.7 %all-reduce.15.cloned.1.call-start = ((), (), s32[]{:S(2)}) async-start(), calls=%async_computation.5 | async-start | bytes 2097152 | tf_op jit(solution)/shard_map/psum | solution.py:11
  656.9 137.8 %reduce-scatter.2.cloned.1.call-start = ((), (), s32[]{:S(2)}) async-start(), calls=%async_computation.6 | async-start | bytes 6291456 | tf_op jit(solution)/shard_map/reduce_scatter | solution.py:41
  731.7 245.5 %all-reduce.17.cloned.1.call-start = ((), (), s32[]{:S(2)}) async-start(), calls=%async_computation.7 | async-start | bytes 4194304 | tf_op jit(solution)/shard_map/psum | solution.py:44
Sparse Core Ops, SparseCore 0:
  12.0 224.5 all-reduce.6
  239.6 60.7 all-reduce.8
  310.7 225.0 all-reduce.10
  538.4 116.0 all-reduce.12
  657.3 64.2 all-reduce.14
  731.8 62.8 reduce-scatter.1
  797.3 179.8 all-reduce.16
